TPU v7x, 512 devices: a whole 4x4x16 slice. The times are simulated.
512 devices in a mesh: dp: 32 (over z, x_hi), mp: 16 (over x_lo, y, core).
Axes of the slice: x: 4 (x_hi: 2, x_lo: 2; x = x_hi * 2 + x_lo), y: 4, z: 16, core: 2. Of those that a mesh axis runs over, the one named last changes fastest.
Arguments:
- tokens: bfloat16 [32768, 2048], P('dp', 'mp'), may hold values from -6 to 6
- norm_gain: bfloat16 [2048], replicated, may hold values from 0.099609375 to 1.8984375
- wi_gate: bfloat16 [2048, 5120], P(None, 'mp'), may hold values from -0.125 to 0.125
- wi_linear: bfloat16 [2048, 5120], P(None, 'mp'), may hold values from -0.125 to 0.125
- wo_out: bfloat16 [5120, 2048], P('mp'), may hold values from -0.078125 to 0.078125
- task_table: float32 [8, 64], replicated, may hold values from -5 to 5
- layer_table: float32 [24, 64], replicated, may hold values from -5 to 5
- task_ids: int32 [256], P('dp'), may hold values from 0 to 7
- layer_index: int32 [1], replicated, may hold values from 0 to 23
- hyper_in: bfloat16 [128, 1024], P(None, 'mp'), may hold values from -0.5 to 0.5
- gen_down: bfloat16 [1024, 131072], P(None, ('mp', 'dp')), may hold values from -0.0078125 to 0.0078125
- gen_up: bfloat16 [1024, 131072], P(None, ('mp', 'dp')), may hold values from -0.046875 to 0.046875
Outputs:
- mixed: bfloat16 [32768, 2048], P('dp', 'mp')
All inputs are finite; a program needn't handle non-finite values.
Results may differ from a plain program's by a relative error of at most 0.019.
Values may be sent and summed in bfloat16 or wider, within the bound.
No kernel may reach another device: no remote copies, remote signals or barrier semaphores. Data moves between devices by JAX's collectives and lax.ppermute only.
A program may use at most 64 MiB of HBM per device.

v0:
```python
import jax
import jax.numpy as jnp
from jax import lax
from jax.sharding import PartitionSpec as P

R = 64


def laid_out(blocks, dim):
    lengths = list(blocks.shape[1:])
    lengths[dim] *= blocks.shape[0]
    return jnp.moveaxis(blocks, 0, dim).reshape(lengths)


def from_everyone(shard, axis):
    copies = jnp.broadcast_to(shard, (lax.axis_size(axis), *shard.shape))
    return lax.all_to_all(copies, axis, split_axis=0, concat_axis=0, tiled=True)


def gather_directly(shard, axis, dim):
    return laid_out(from_everyone(shard, axis), dim)


def of_everyone(shard, axis):
    everything = from_everyone(shard, axis)
    return jnp.sum(everything.astype(jnp.float32), axis=0)


def matmul(left, right):
    return jnp.dot(left, right, preferred_element_type=jnp.float32)


def per_device(
    tokens,
    norm_gain,
    wi_gate,
    wi_linear,
    wo_out,
    task_table,
    layer_table,
    task_ids,
    layer_index,
    hyper_in,
    gen_down,
    gen_up,
):
    task_count = task_table.shape[0]
    layer_row = jnp.take(layer_table, layer_index, axis=0)
    embed = jnp.concatenate(
        [task_table, jnp.broadcast_to(layer_row, (task_count, layer_row.shape[1]))], axis=1
    ).astype(jnp.bfloat16)
    hidden_part = jnp.maximum(matmul(embed, hyper_in), 0.0).astype(jnp.bfloat16)
    hidden = gather_directly(hidden_part, "mp", 1)
    every_id = gather_directly(task_ids, "dp", 0)
    wanted = jnp.take(hidden, every_id, axis=0)
    made = (
        matmul(wanted, gen_down).astype(jnp.bfloat16),
        matmul(wanted, gen_up).astype(jnp.bfloat16),
    )
    local_down, local_up = (
        lax.all_to_all(made[0], "dp", split_axis=0, concat_axis=1, tiled=True),
        lax.all_to_all(made[1], "dp", split_axis=0, concat_axis=1, tiled=True),
    )
    full_rows = lax.all_gather(tokens, "mp", axis=1, tiled=True)
    wide = full_rows.astype(jnp.float32)
    scale = lax.rsqrt(jnp.mean(wide * wide, axis=-1, keepdims=True) + 1e-06)
    normed = (wide * scale * norm_gain.astype(jnp.float32)).astype(jnp.bfloat16)
    gate = matmul(normed, wi_gate)
    linear = matmul(normed, wi_linear)
    act = (jax.nn.gelu(gate, approximate=True) * linear).astype(jnp.bfloat16)
    seqs_dev = task_ids.shape[0]
    tok_dev = tokens.shape[0]
    seq_len = tok_dev // seqs_dev
    partial_sums = matmul(act, wo_out)
    ffout = lax.psum_scatter(
        partial_sums.astype(jnp.bfloat16), "mp", scatter_dimension=1, tiled=True
    )
    down_block = local_down.reshape(seqs_dev, -1, R)
    up_block = local_up.reshape(seqs_dev, -1, R)
    blocks = ffout.reshape(seqs_dev, seq_len, -1)
    squeeze_part = jnp.einsum(
        "std,sdr->str", blocks, down_block, preferred_element_type=jnp.float32
    )
    squeeze_full = of_everyone(squeeze_part.astype(jnp.bfloat16), "mp").astype(jnp.float32)
    squeezed = jnp.maximum(squeeze_full, 0.0).astype(jnp.bfloat16)
    expand = jnp.einsum("str,sdr->std", squeezed, up_block, preferred_element_type=jnp.float32)
    total = tokens.astype(jnp.float32) + ffout.astype(jnp.float32) + expand.reshape(tok_dev, -1)
    return total.astype(jnp.bfloat16)


def solution(mesh):
    return jax.shard_map(
        per_device,
        mesh=mesh,
        in_specs=(
            P("dp", "mp"),
            P(),
            P(None, "mp"),
            P(None, "mp"),
            P("mp", None),
            P(),
            P(),
            P("dp"),
            P(),
            P(None, "mp"),
            P(None, ("mp", "dp")),
            P(None, ("mp", "dp")),
        ),
        out_specs=P("dp", "mp"),
        check_vma=False,
    )
```

profile of v0, /device:TPU:25, one launch (start us, length us, event | category | flops | bytes accessed | tf_op | source)
XLA Modules:
  0.0 219.2 jit_solution(13709303609028139173)
XLA Ops:
  6.5 0.7 all-gather.2.cloned.1.call-update
  7.3 0.0 reduce-scatter.4.cloned.1.call-start
  7.3 0.7 convert_element_type.45
  8.0 58.1 %all-gather.2.cloned.1.call-done = bf16[1024,2048]{1,0:T(8,128)(2,1)} async-done(((bf16[1024,128]{1,0:T(8,128)(2,1)}), bf16[1024,2048]{1,0:T(8,128)(2,1)}) %all-gather.2.cloned.1.call-update) | async-done | bytes 4194320 | tf_op jit(solution)/shard_map/all_gather | solution.py:64
  66.1 3.2 %fusion = f32[1024]{0:T(1024)S(1)} fusion(bf16[1024,2048]{1,0:T(8,128)(2,1)} %all-gather.2.cloned.1.call-done), kind=kLoop, calls=%fused_computation.3 | loop fusion | flops 6290432 | bytes 4198400 | tf_op jit(solution)/shard_map/reduce_sum | solution.py:66
  69.3 0.2 copy-done.1
  69.5 4.2 %fusion.12 = f32[1024,320]{0,1:T(8,128)} fusion(bf16[2048,320]{0,1:T(8,128)(2,1)} %param.14, bf16[1024,2048]{1,0:T(8,128)(2,1)S(1)} %copy-done.1, f32[2048]{0:T(1024)S(1)} %convert_element_type.45, f32[1024]{0:T(1024)S(1)} %add_rsqrt_fusion), kind=kOutput, calls=%fused_computation.18 | convolution fusion | flops 1350565888 | bytes 6828032 | tf_op jit(solution)/shard_map/dot_general | solution.py:30
  73.8 8.6 %convolution_convert_fusion = bf16[1024,2048]{1,0:T(8,128)(2,1)} fusion(bf16[320,2048]{1,0:T(8,128)(2,1)S(1)} %copy-done, bf16[2048,320]{0,1:T(8,128)(2,1)S(1)} %copy-done.10, f32[1024,320]{0,1:T(8,128)} %fusion.12, bf16[1024,2048]{1,0:T(8,128)(2,1)} %all-gather.2.cloned.1.call-done, f32[2048]{0:T(1024)S(1)} %convert_element_type.45, f32[1024]{0:T(1024)S(1)} %add_rsqrt_fusion), kind=kOutput, calls=%fused_computation.7 | convolution fusion | flops 2698117120 | bytes 12333056 | tf_op jit(solution)/shard_map/dot_general | solution.py:30
  82.4 6.4 %copy.23 = bf16[1024,2048]{0,1:T(8,128)(2,1)} copy(bf16[1024,2048]{1,0:T(8,128)(2,1)} %convolution_convert_fusion) | data formatting | bytes 8388608
  88.8 0.0 reduce-scatter.4.cloned.1.call-update
  88.8 0.6 copy-done.9
  89.4 0.6 broadcast_in_dim.38
  90.0 14.2 %all-to-all-start = ((s32[32,1,8]{2,1,0:T(1,128)}), s32[32,1,8]{2,1,0:T(1,128)S(1)}, u32[]{:S(2)}, u32[]{:S(2)}) async-start(s32[32,1,8]{2,1,0:T(1,128)} %broadcast_in_dim.38), calls=%async_computation | async-start | bytes 32768 | tf_op jit(solution)/shard_map/all_to_all | solution.py:17
  105.0 0.7 fusion.30
  105.7 0.1 pad.3.clone
  105.7 0.1 fusion.18
  105.9 0.7 reshape.145
  106.6 11.3 %all-to-all-done = s32[32,1,8]{2,1,0:T(1,128)S(1)} async-done(((s32[32,1,8]{2,1,0:T(1,128)}), s32[32,1,8]{2,1,0:T(1,128)S(1)}, u32[]{:S(2)}, u32[]{:S(2)}) %all-to-all-start) | async-done | bytes 1056 | tf_op jit(solution)/shard_map/all_to_all | solution.py:17
  117.9 6.1 %all-to-all-start.1 = ((bf16[16,2,256]{2,1,0:T(2,128)(2,1)}), bf16[16,2,256]{2,1,0:T(2,128)(2,1)S(1)}, u32[]{:S(2)}, u32[]{:S(2)}) async-start(bf16[16,2,256]{2,1,0:T(2,128)(2,1)} %reshape.145), calls=%async_computation.1 | async-start | bytes 32768 | tf_op jit(solution)/shard_map/all_to_all | solution.py:17
  124.0 0.1 reshape.91
  124.1 0.6 broadcast.82
  124.7 0.7 reduce.5
  125.4 0.1 reshape.89
  125.6 2.6 %all-to-all-done.1 = bf16[16,2,256]{2,1,0:T(2,128)(2,1)S(1)} async-done(((bf16[16,2,256]{2,1,0:T(2,128)(2,1)}), bf16[16,2,256]{2,1,0:T(2,128)(2,1)S(1)}, u32[]{:S(2)}, u32[]{:S(2)}) %all-to-all-start.1) | async-done | bytes 16416 | tf_op jit(solution)/shard_map/all_to_all | solution.py:17
  128.2 0.1 reshape.146
  128.3 0.1 reshape.90
  128.4 0.0 copy-start.11
  128.4 1.2 gather_fusion
  129.6 0.0 copy-start.12
  129.6 1.0 fusion.14
  130.6 3.8 %all-to-all-start.2 = ((bf16[32,8,256]{2,1,0:T(8,128)(2,1)}), bf16[32,8,256]{2,1,0:T(8,128)(2,1)S(1)}, u32[]{:S(2)}, u32[]{:S(2)}) async-start(bf16[32,8,256]{2,1,0:T(8,128)(2,1)} %fusion.14), calls=%async_computation.2 | async-start | bytes 262144 | tf_op jit(solution)/shard_map/all_to_all | solution.py:61
  134.4 1.0 fusion.15
  135.4 14.6 %all-to-all-done.2 = bf16[32,8,256]{2,1,0:T(8,128)(2,1)S(1)} async-done(((bf16[32,8,256]{2,1,0:T(8,128)(2,1)}), bf16[32,8,256]{2,1,0:T(8,128)(2,1)S(1)}, u32[]{:S(2)}, u32[]{:S(2)}) %all-to-all-start.2) | async-done | bytes 131104 | tf_op jit(solution)/shard_map/all_to_all | solution.py:61
  150.0 5.2 %all-to-all-start.4 = ((bf16[32,8,256]{2,1,0:T(8,128)(2,1)}), bf16[32,8,256]{2,1,0:T(8,128)(2,1)S(1)}, u32[]{:S(2)}, u32[]{:S(2)}) async-start(bf16[32,8,256]{2,1,0:T(8,128)(2,1)} %fusion.15), calls=%async_computation.4 | async-start | bytes 262144 | tf_op jit(solution)/shard_map/all_to_all | solution.py:62
  155.3 0.2 reshape.92
  155.4 7.9 %reduce-scatter.4.cloned.1.call-done = bf16[128,1024]{1,0:T(8,128)(2,1)} async-done(((bf16[2048,1024]{1,0:T(8,128)(2,1)}), bf16[128,1024]{1,0:T(8,128)(2,1)}) %reduce-scatter.4.cloned.1.call-update) | async-done | bytes 262160
  163.4 1.1 copy.24
  164.5 0.3 convolution_convert_fusion.2
  164.8 5.2 %all-to-all-done.4 = bf16[32,8,256]{2,1,0:T(8,128)(2,1)S(1)} async-done(((bf16[32,8,256]{2,1,0:T(8,128)(2,1)}), bf16[32,8,256]{2,1,0:T(8,128)(2,1)S(1)}, u32[]{:S(2)}, u32[]{:S(2)}) %all-to-all-start.4) | async-done | bytes 131104 | tf_op jit(solution)/shard_map/all_to_all | solution.py:62
  170.0 1.9 broadcast_in_dim.46
  171.9 8.9 %all-to-all-start.3 = ((bf16[16,8,128,64]{2,3,1,0:T(8,128)(2,1)}), bf16[16,8,128,64]{2,3,1,0:T(8,128)(2,1)S(1)}, u32[]{:S(2)}, u32[]{:S(2)}) async-start(bf16[16,8,128,64]{2,3,1,0:T(8,128)(2,1)} %broadcast_in_dim.46), calls=%async_computation.3 | async-start | bytes 4194304 | tf_op jit(solution)/shard_map/all_to_all | solution.py:17
  180.8 0.9 copy.19
  181.7 0.9 reshape.93
  182.6 27.8 %all-to-all-done.3 = bf16[16,8,128,64]{2,3,1,0:T(8,128)(2,1)S(1)} async-done(((bf16[16,8,128,64]{2,3,1,0:T(8,128)(2,1)}), bf16[16,8,128,64]{2,3,1,0:T(8,128)(2,1)S(1)}, u32[]{:S(2)}, u32[]{:S(2)}) %all-to-all-start.3) | async-done | bytes 2097184 | tf_op jit(solution)/shard_map/all_to_all | solution.py:17
  210.3 0.3 convert_reduce_fusion
  210.7 0.6 copy-done.5
  211.3 0.3 fusion.24
  211.6 0.8 fusion.23
  (30 shorter events, 0.1 us)
Async XLA Ops:
  6.5 67.2 %copy-start = (bf16[320,2048]{1,0:T(8,128)(2,1)S(1)}, bf16[320,2048]{1,0:T(8,128)(2,1)}, u32[]{:S(2)}) copy-start(bf16[320,2048]{1,0:T(8,128)(2,1)} %param.16) | copy-start | bytes 3932164
  6.5 59.6 %all-gather.2.cloned.1.call-start = ((), (), s32[]{:S(2)}) async-start(), calls=%async_computation.6 | async-start | bytes 4456448 | tf_op jit(solution)/shard_map/all_gather | solution.py:64
  7.3 156.1 %reduce-scatter.4.cloned.1.call-start = ((), (), s32[]{:S(2)}) async-start(), calls=%async_computation.7 | async-start | bytes 4456448
  66.1 3.4 %copy-start.1 = (bf16[1024,2048]{1,0:T(8,128)(2,1)S(1)}, bf16[1024,2048]{1,0:T(8,128)(2,1)}, u32[]{:S(2)}) copy-start(bf16[1024,2048]{1,0:T(8,128)(2,1)} %all-gather.2.cloned.1.call-done) | copy-start | bytes 12582916
  69.5 4.2 %copy-start.10 = (bf16[2048,320]{0,1:T(8,128)(2,1)S(1)}, bf16[2048,320]{0,1:T(8,128)(2,1)}, u32[]{:S(2)}) copy-start(bf16[2048,320]{0,1:T(8,128)(2,1)} %param.15) | copy-start | bytes 3932164
  88.8 0.7 copy-start.9
  88.8 16.2 %copy-start.8 = (f32[8,64]{1,0:T(8,128)S(1)}, f32[8,64]{1,0:T(8,128)}, u32[]{:S(2)}) copy-start(f32[8,64]{1,0:T(8,128)} %param.17) | copy-start | bytes 6148
  88.8 17.0 %copy-start.7 = (bf16[128,64]{0,1:T(8,128)(2,1)S(1)}, bf16[128,64]{0,1:T(8,128)(2,1)}, u32[]{:S(2)}) copy-start(bf16[128,64]{0,1:T(8,128)(2,1)} %param.21) | copy-start | bytes 49156
  90.0 27.9 %all-to-all-start = ((s32[32,1,8]{2,1,0:T(1,128)}), s32[32,1,8]{2,1,0:T(1,128)S(1)}, u32[]{:S(2)}, u32[]{:S(2)}) async-start(s32[32,1,8]{2,1,0:T(1,128)} %broadcast_in_dim.38), calls=%async_computation | async-start | bytes 32768 | tf_op jit(solution)/shard_map/all_to_all | solution.py:17
  117.9 10.2 %all-to-all-start.1 = ((bf16[16,2,256]{2,1,0:T(2,128)(2,1)}), bf16[16,2,256]{2,1,0:T(2,128)(2,1)S(1)}, u32[]{:S(2)}, u32[]{:S(2)}) async-start(bf16[16,2,256]{2,1,0:T(2,128)(2,1)} %reshape.145), calls=%async_computation.1 | async-start | bytes 32768 | tf_op jit(solution)/shard_map/all_to_all | solution.py:17
  128.4 1.2 copy-start.11
  129.6 4.9 %copy-start.12 = (bf16[1024,256]{1,0:T(8,128)(2,1)S(1)}, bf16[1024,256]{1,0:T(8,128)(2,1)}, u32[]{:S(2)}) copy-start(bf16[1024,256]{1,0:T(8,128)(2,1)} %param.23) | copy-start | bytes 1572868
  130.6 19.4 %all-to-all-start.2 = ((bf16[32,8,256]{2,1,0:T(8,128)(2,1)}), bf16[32,8,256]{2,1,0:T(8,128)(2,1)S(1)}, u32[]{:S(2)}, u32[]{:S(2)}) async-start(bf16[32,8,256]{2,1,0:T(8,128)(2,1)} %fusion.14), calls=%async_computation.2 | async-start | bytes 262144 | tf_op jit(solution)/shard_map/all_to_all | solution.py:61
  150.0 20.0 %all-to-all-start.4 = ((bf16[32,8,256]{2,1,0:T(8,128)(2,1)}), bf16[32,8,256]{2,1,0:T(8,128)(2,1)S(1)}, u32[]{:S(2)}, u32[]{:S(2)}) async-start(bf16[32,8,256]{2,1,0:T(8,128)(2,1)} %fusion.15), calls=%async_computation.4 | async-start | bytes 262144 | tf_op jit(solution)/shard_map/all_to_all | solution.py:62
  164.5 7.4 %copy-start.2 = (bf16[1024,128]{1,0:T(8,128)(2,1)}, bf16[1024,128]{1,0:T(8,128)(2,1)S(1)}, u32[]{:S(2)}) copy-start(bf16[1024,128]{1,0:T(8,128)(2,1)S(1)} %copy.24) | copy-start | bytes 786436
  170.0 1.9 copy-start.6
  171.9 38.4 %all-to-all-start.3 = ((bf16[16,8,128,64]{2,3,1,0:T(8,128)(2,1)}), bf16[16,8,128,64]{2,3,1,0:T(8,128)(2,1)S(1)}, u32[]{:S(2)}, u32[]{:S(2)}) async-start(bf16[16,8,128,64]{2,3,1,0:T(8,128)(2,1)} %broadcast_in_dim.46), calls=%async_computation.3 | async-start | bytes 4194304 | tf_op jit(solution)/shard_map/all_to_all | solution.py:17
  210.3 1.0 copy-start.5
  210.3 1.3 copy-start.3
  210.3 1.3 copy-start.4
Sparse Core Ops, SparseCore 0:
  9.4 56.6 all-gather.1
  88.9 74.3 reduce-scatter.3
where the time goes:
time: 220 us; the launch traced here: 219 us
  waiting for transfers between devices  128 us (58%)
  starting transfers between devices  38.3 us (17%)
  local copies, waits for them, and re-layouts  16.4 us (7%)
  matrix products  15.6 us (7%)
  between operations  14.2 us (6%)
  other arithmetic  6.5 us (3%)
    all_gather x1, waiting for transfers between devices, per_device(): full_rows = lax.all_gather(tokens, 'mp', axis=1, tiled=True)  58.1 us
    all_to_all x3, waiting for transfers between devices, from_everyone(): return lax.all_to_all(copies, axis, split_axis=0, concat_axis=0, tiled=True)  41.7 us
    all_to_all x3, starting transfers between devices, from_everyone(): return lax.all_to_all(copies, axis, split_axis=0, concat_axis=0, tiled=True)  29.2 us
    dot_general x5, matrix products, matmul(): return jnp.dot(left, right, preferred_element_type=jnp.float32)  15 us
    all_to_all x1, waiting for transfers between devices, per_device(): lax.all_to_all(made[0], 'dp', split_axis=0, concat_axis=1, tiled=True)  14.6 us
    unnamed x30, local copies, waits for them, and re-layouts  9.83 us
    unnamed x3, waiting for transfers between devices  8.67 us
    all_to_all x1, starting transfers between devices, per_device(): lax.all_to_all(made[1], 'dp', split_axis=0, concat_axis=1, tiled=True)  5.21 us
  transfers between devices with their start and end apart: 7, of which 7 were waited for; matrix products, arithmetic and copies ran while one was open for 5% of the time, Pallas kernels for 0%

commit v1 on v0

--- a/solution.py
+++ b/solution.py
@@ -61,7 +61,9 @@
         lax.all_to_all(made[0], "dp", split_axis=0, concat_axis=1, tiled=True),
         lax.all_to_all(made[1], "dp", split_axis=0, concat_axis=1, tiled=True),
     )
-    full_rows = lax.all_gather(tokens, "mp", axis=1, tiled=True)
+    full_rows = jnp.concatenate(
+        lax.all_to_all(jnp.stack([tokens] * lax.axis_size("mp")), "mp", 0, 0), axis=1
+    )
     wide = full_rows.astype(jnp.float32)
     scale = lax.rsqrt(jnp.mean(wide * wide, axis=-1, keepdims=True) + 1e-06)
     normed = (wide * scale * norm_gain.astype(jnp.float32)).astype(jnp.bfloat16)

time: 220 us -> 238 us (1.082)
  starting transfers between devices: 38.3 us -> 48.2 us
  local copies, waits for them, and re-layouts: 16.4 us -> 21.8 us
  waiting for transfers between devices: 128 us -> 131 us
    all_to_all x0 -> x1, waiting for transfers between devices: none -> 61.5 us  [per_device(): lax.all_to_all(jnp.stack([tokens] * lax.axis_size('mp')), 'mp', 0, 0)]
    all_gather x1 -> x0, waiting for transfers between devices: 58.1 us -> none  [per_device(): full_rows = lax.all_gather(tokens, 'mp', axis=1, tiled=True)]
    all_to_all x0 -> x1, starting transfers between devices: none -> 10.3 us  [per_device(): lax.all_to_all(jnp.stack([tokens] * lax.axis_size('mp')), 'mp', 0, 0)]
    unnamed x30 -> x35, local copies, waits for them, and re-layouts: 9.83 us -> 12.8 us
    another operation x0 -> x1, local copies, waits for them, and re-layouts: none -> 2.52 us  [per_device(): jnp.stack([tokens] * lax.axis_size('mp'))]
    unnamed x3 -> x2, waiting for transfers between devices: 8.67 us -> 7.69 us
  transfers between devices with their start and end apart: 7 -> 7, of which waited for: 7 -> 7; matrix products, arithmetic and copies ran while one was open for 5% -> 4% of each run, Pallas kernels for 0% -> 0%
where the time goes in v1:
time: 238 us; the launch traced here: 237 us
  waiting for transfers between devices  131 us (55%)
  starting transfers between devices  48.2 us (20%)
  local copies, waits for them, and re-layouts  21.8 us (9%)
  between operations  14.3 us (6%)
  matrix products  13.9 us (6%)
  other arithmetic  8.45 us (4%)
    all_to_all x1, waiting for transfers between devices, per_device(): lax.all_to_all(jnp.stack([tokens] * lax.axis_size('mp')), 'mp', 0, 0)  61.5 us
    all_to_all x3, waiting for transfers between devices, from_everyone(): return lax.all_to_all(copies, axis, split_axis=0, concat_axis=0, tiled=True)  41.8 us
    all_to_all x3, starting transfers between devices, from_everyone(): return lax.all_to_all(copies, axis, split_axis=0, concat_axis=0, tiled=True)  28.3 us
    all_to_all x1, waiting for transfers between devices, per_device(): lax.all_to_all(made[0], 'dp', split_axis=0, concat_axis=1, tiled=True)  14.1 us
    dot_general x5, matrix products, matmul(): return jnp.dot(left, right, preferred_element_type=jnp.float32)  13.3 us
    unnamed x35, local copies, waits for them, and re-layouts  12.8 us
    all_to_all x1, starting transfers between devices, per_device(): lax.all_to_all(jnp.stack([tokens] * lax.axis_size('mp')), 'mp', 0, 0)  10.3 us
    unnamed x2, waiting for transfers between devices  7.69 us
  transfers between devices with their start and end apart: 7, of which 7 were waited for; matrix products, arithmetic and copies ran while one was open for 4% of the time, Pallas kernels for 0%

profile of v1, /device:TPU:25, one launch (start us, length us, event | category | flops | bytes accessed | tf_op | source)
XLA Modules:
  0.0 237.1 jit_solution(6015576309951389350)
XLA Ops:
  6.5 1.2 copy.17
  7.7 2.5 %stack.2 = bf16[16,1024,128]{1,2,0:T(8,128)(2,1)} broadcast(bf16[1024,128]{0,1:T(8,128)(2,1)S(1)} %copy.17), dimensions={1,2} | broadcast | bytes 4456448 | tf_op jit(solution)/shard_map/stack | solution.py:65
  10.3 10.3 %all-to-all-start = ((bf16[16,1024,128]{1,2,0:T(8,128)(2,1)}), bf16[16,1024,128]{1,2,0:T(8,128)(2,1)}, u32[]{:S(2)}, u32[]{:S(2)}) async-start(bf16[16,1024,128]{1,2,0:T(8,128)(2,1)} %stack.2), calls=%async_computation | async-start | bytes 8388608 | tf_op jit(solution)/shard_map/all_to_all | solution.py:65
  20.6 0.0 reduce-scatter.4.cloned.1.call-start
  20.7 61.5 %all-to-all-done = bf16[16,1024,128]{1,2,0:T(8,128)(2,1)} async-done(((bf16[16,1024,128]{1,2,0:T(8,128)(2,1)}), bf16[16,1024,128]{1,2,0:T(8,128)(2,1)}, u32[]{:S(2)}, u32[]{:S(2)}) %all-to-all-start) | async-done | bytes 4194336 | tf_op jit(solution)/shard_map/all_to_all | solution.py:65
  82.2 3.1 %multiply_reduce_fusion = f32[1024]{0:T(1024)S(1)} fusion(bf16[16,1024,128]{1,2,0:T(8,128)(2,1)} %all-to-all-done), kind=kLoop, calls=%fused_computation.4 | loop fusion | flops 6290432 | bytes 4198400 | tf_op jit(solution)/shard_map/reduce_sum | solution.py:68
  85.3 2.9 %fusion.1 = bf16[1024,2048]{0,1:T(8,128)(2,1)S(1)} fusion(f32[2048]{0:T(1024)S(1)} %convert_element_type.58, f32[1024]{0:T(1024)S(1)} %add_rsqrt_fusion, bf16[16,1024,128]{1,2,0:T(8,128)(2,1)} %all-to-all-done), kind=kLoop, calls=%fused_computation.3 | loop fusion | flops 8388608 | bytes 8400896 | tf_op jit(solution)/shard_map/convert_element_type | solution.py:69
  88.2 1.9 copy-done.1
  90.2 2.7 %fusion.33 = f32[1024,320]{0,1:T(8,128)} fusion(bf16[2048,320]{0,1:T(8,128)(2,1)S(1)} %copy-done.11, bf16[1024,2048]{0,1:T(8,128)(2,1)S(1)} %fusion.1), kind=kOutput, calls=%fused_computation.53 | convolution fusion | flops 1342177280 | bytes 6815744 | tf_op jit(solution)/shard_map/dot_general | solution.py:30
  92.9 8.4 %convolution_convert_fusion = bf16[1024,2048]{1,0:T(8,128)(2,1)} fusion(bf16[320,2048]{1,0:T(8,128)(2,1)S(1)} %copy-done, bf16[2048,320]{0,1:T(8,128)(2,1)S(1)} %copy-done.12, bf16[1024,2048]{0,1:T(8,128)(2,1)} %copy-done.1, f32[1024,320]{0,1:T(8,128)} %fusion.33), kind=kOutput, calls=%fused_computation.6 | convolution fusion | flops 2689728512 | bytes 12320768 | tf_op jit(solution)/shard_map/dot_general | solution.py:30
  101.3 6.4 %copy.25 = bf16[1024,2048]{0,1:T(8,128)(2,1)} copy(bf16[1024,2048]{1,0:T(8,128)(2,1)} %convolution_convert_fusion) | data formatting | bytes 8388608
  107.7 0.0 reduce-scatter.4.cloned.1.call-update
  107.7 0.6 copy-done.10
  108.4 0.6 broadcast_in_dim.38
  109.0 13.1 %all-to-all-start.1 = ((s32[32,1,8]{2,1,0:T(1,128)}), s32[32,1,8]{2,1,0:T(1,128)S(1)}, u32[]{:S(2)}, u32[]{:S(2)}) async-start(s32[32,1,8]{2,1,0:T(1,128)} %broadcast_in_dim.38), calls=%async_computation.1 | async-start | bytes 32768 | tf_op jit(solution)/shard_map/all_to_all | solution.py:17
  122.8 0.7 fusion.24
  123.5 0.1 pad.3.clone
  123.6 0.1 fusion.12
  123.7 0.7 reshape.152
  124.4 11.2 %all-to-all-done.1 = s32[32,1,8]{2,1,0:T(1,128)S(1)} async-done(((s32[32,1,8]{2,1,0:T(1,128)}), s32[32,1,8]{2,1,0:T(1,128)S(1)}, u32[]{:S(2)}, u32[]{:S(2)}) %all-to-all-start.1) | async-done | bytes 1056 | tf_op jit(solution)/shard_map/all_to_all | solution.py:17
  135.7 6.3 %all-to-all-start.2 = ((bf16[16,2,256]{2,1,0:T(2,128)(2,1)}), bf16[16,2,256]{2,1,0:T(2,128)(2,1)S(1)}, u32[]{:S(2)}, u32[]{:S(2)}) async-start(bf16[16,2,256]{2,1,0:T(2,128)(2,1)} %reshape.152), calls=%async_computation.2 | async-start | bytes 32768 | tf_op jit(solution)/shard_map/all_to_all | solution.py:17
  141.9 0.1 reshape.97
  142.0 0.5 broadcast.84
  142.5 0.6 reduce.7
  143.1 0.1 reshape.95
  143.3 2.8 %all-to-all-done.2 = bf16[16,2,256]{2,1,0:T(2,128)(2,1)S(1)} async-done(((bf16[16,2,256]{2,1,0:T(2,128)(2,1)}), bf16[16,2,256]{2,1,0:T(2,128)(2,1)S(1)}, u32[]{:S(2)}, u32[]{:S(2)}) %all-to-all-start.2) | async-done | bytes 16416 | tf_op jit(solution)/shard_map/all_to_all | solution.py:17
  146.0 0.1 reshape.153
  146.1 0.1 reshape.96
  146.3 1.2 gather_fusion
  147.4 1.0 fusion.10
  148.5 3.9 %all-to-all-start.3 = ((bf16[32,8,256]{2,1,0:T(8,128)(2,1)}), bf16[32,8,256]{2,1,0:T(8,128)(2,1)S(1)}, u32[]{:S(2)}, u32[]{:S(2)}) async-start(bf16[32,8,256]{2,1,0:T(8,128)(2,1)} %fusion.10), calls=%async_computation.3 | async-start | bytes 262144 | tf_op jit(solution)/shard_map/all_to_all | solution.py:61
  152.3 1.0 fusion.11
  153.3 14.1 %all-to-all-done.3 = bf16[32,8,256]{2,1,0:T(8,128)(2,1)S(1)} async-done(((bf16[32,8,256]{2,1,0:T(8,128)(2,1)}), bf16[32,8,256]{2,1,0:T(8,128)(2,1)S(1)}, u32[]{:S(2)}, u32[]{:S(2)}) %all-to-all-start.3) | async-done | bytes 131104 | tf_op jit(solution)/shard_map/all_to_all | solution.py:61
  167.4 5.7 %all-to-all-start.5 = ((bf16[32,8,256]{2,1,0:T(8,128)(2,1)}), bf16[32,8,256]{2,1,0:T(8,128)(2,1)S(1)}, u32[]{:S(2)}, u32[]{:S(2)}) async-start(bf16[32,8,256]{2,1,0:T(8,128)(2,1)} %fusion.11), calls=%async_computation.5 | async-start | bytes 262144 | tf_op jit(solution)/shard_map/all_to_all | solution.py:62
  173.1 0.2 reshape.98
  173.3 7.7 %reduce-scatter.4.cloned.1.call-done = bf16[128,1024]{1,0:T(8,128)(2,1)} async-done(((bf16[2048,1024]{1,0:T(8,128)(2,1)}), bf16[128,1024]{1,0:T(8,128)(2,1)}) %reduce-scatter.4.cloned.1.call-update) | async-done | bytes 262160
  181.0 1.1 copy.26
  182.1 0.3 convolution_convert_fusion.2
  182.4 5.5 %all-to-all-done.5 = bf16[32,8,256]{2,1,0:T(8,128)(2,1)S(1)} async-done(((bf16[32,8,256]{2,1,0:T(8,128)(2,1)}), bf16[32,8,256]{2,1,0:T(8,128)(2,1)S(1)}, u32[]{:S(2)}, u32[]{:S(2)}) %all-to-all-start.5) | async-done | bytes 131104 | tf_op jit(solution)/shard_map/all_to_all | solution.py:62
  187.9 1.9 broadcast_in_dim.46
  189.7 8.9 %all-to-all-start.4 = ((bf16[16,8,128,64]{2,3,1,0:T(8,128)(2,1)}), bf16[16,8,128,64]{2,3,1,0:T(8,128)(2,1)S(1)}, u32[]{:S(2)}, u32[]{:S(2)}) async-start(bf16[16,8,128,64]{2,3,1,0:T(8,128)(2,1)} %broadcast_in_dim.46), calls=%async_computation.4 | async-start | bytes 4194304 | tf_op jit(solution)/shard_map/all_to_all | solution.py:17
  198.6 0.9 copy.21
  199.6 0.9 reshape.99
  200.4 27.8 %all-to-all-done.4 = bf16[16,8,128,64]{2,3,1,0:T(8,128)(2,1)S(1)} async-done(((bf16[16,8,128,64]{2,3,1,0:T(8,128)(2,1)}), bf16[16,8,128,64]{2,3,1,0:T(8,128)(2,1)S(1)}, u32[]{:S(2)}, u32[]{:S(2)}) %all-to-all-start.4) | async-done | bytes 2097184 | tf_op jit(solution)/shard_map/all_to_all | solution.py:17
  228.2 0.3 convert_reduce_fusion
  228.5 0.6 copy-done.5
  229.1 0.3 fusion.18
  229.5 0.8 fusion.17
  (36 shorter events, 0.1 us)
Async XLA Ops:
  6.5 86.4 %copy-start = (bf16[320,2048]{1,0:T(8,128)(2,1)S(1)}, bf16[320,2048]{1,0:T(8,128)(2,1)}, u32[]{:S(2)}) copy-start(bf16[320,2048]{1,0:T(8,128)(2,1)} %param.16) | copy-start | bytes 3932164
  10.3 10.4 %copy-start.8 = (bf16[2048]{0:T(1024)(128)(2,1)S(1)}, bf16[2048]{0:T(1024)(128)(2,1)}, u32[]{:S(2)}) copy-start(bf16[2048]{0:T(1024)(128)(2,1)} %param.13) | copy-start | bytes 12292
  10.3 72.0 %all-to-all-start = ((bf16[16,1024,128]{1,2,0:T(8,128)(2,1)}), bf16[16,1024,128]{1,2,0:T(8,128)(2,1)}, u32[]{:S(2)}, u32[]{:S(2)}) async-start(bf16[16,1024,128]{1,2,0:T(8,128)(2,1)} %stack.2), calls=%async_computation | async-start | bytes 8388608 | tf_op jit(solution)/shard_map/all_to_all | solution.py:65
  20.6 160.4 %reduce-scatter.4.cloned.1.call-start = ((), (), s32[]{:S(2)}) async-start(), calls=%async_computation.7 | async-start | bytes 4456448
  85.3 4.8 %copy-start.11 = (bf16[2048,320]{0,1:T(8,128)(2,1)S(1)}, bf16[2048,320]{0,1:T(8,128)(2,1)}, u32[]{:S(2)}) copy-start(bf16[2048,320]{0,1:T(8,128)(2,1)} %param.14) | copy-start | bytes 3932164
  88.2 2.0 copy-start.1
  90.2 2.7 %copy-start.12 = (bf16[2048,320]{0,1:T(8,128)(2,1)S(1)}, bf16[2048,320]{0,1:T(8,128)(2,1)}, u32[]{:S(2)}) copy-start(bf16[2048,320]{0,1:T(8,128)(2,1)} %param.15) | copy-start | bytes 3932164
  107.7 0.7 copy-start.10
  107.7 15.0 %copy-start.9 = (f32[8,64]{1,0:T(8,128)S(1)}, f32[8,64]{1,0:T(8,128)}, u32[]{:S(2)}) copy-start(f32[8,64]{1,0:T(8,128)} %param.17) | copy-start | bytes 6148
  107.7 15.8 %copy-start.7 = (bf16[128,64]{0,1:T(8,128)(2,1)S(1)}, bf16[128,64]{0,1:T(8,128)(2,1)}, u32[]{:S(2)}) copy-start(bf16[128,64]{0,1:T(8,128)(2,1)} %param.21) | copy-start | bytes 49156
  109.0 26.7 %all-to-all-start.1 = ((s32[32,1,8]{2,1,0:T(1,128)}), s32[32,1,8]{2,1,0:T(1,128)S(1)}, u32[]{:S(2)}, u32[]{:S(2)}) async-start(s32[32,1,8]{2,1,0:T(1,128)} %broadcast_in_dim.38), calls=%async_computation.1 | async-start | bytes 32768 | tf_op jit(solution)/shard_map/all_to_all | solution.py:17
  135.7 10.4 %all-to-all-start.2 = ((bf16[16,2,256]{2,1,0:T(2,128)(2,1)}), bf16[16,2,256]{2,1,0:T(2,128)(2,1)S(1)}, u32[]{:S(2)}, u32[]{:S(2)}) async-start(bf16[16,2,256]{2,1,0:T(2,128)(2,1)} %reshape.152), calls=%async_computation.2 | async-start | bytes 32768 | tf_op jit(solution)/shard_map/all_to_all | solution.py:17
  146.2 1.2 copy-start.13
  147.4 4.9 %copy-start.14 = (bf16[1024,256]{1,0:T(8,128)(2,1)S(1)}, bf16[1024,256]{1,0:T(8,128)(2,1)}, u32[]{:S(2)}) copy-start(bf16[1024,256]{1,0:T(8,128)(2,1)} %param.23) | copy-start | bytes 1572868
  148.5 19.0 %all-to-all-start.3 = ((bf16[32,8,256]{2,1,0:T(8,128)(2,1)}), bf16[32,8,256]{2,1,0:T(8,128)(2,1)S(1)}, u32[]{:S(2)}, u32[]{:S(2)}) async-start(bf16[32,8,256]{2,1,0:T(8,128)(2,1)} %fusion.10), calls=%async_computation.3 | async-start | bytes 262144 | tf_op jit(solution)/shard_map/all_to_all | solution.py:61
  167.4 20.4 %all-to-all-start.5 = ((bf16[32,8,256]{2,1,0:T(8,128)(2,1)}), bf16[32,8,256]{2,1,0:T(8,128)(2,1)S(1)}, u32[]{:S(2)}, u32[]{:S(2)}) async-start(bf16[32,8,256]{2,1,0:T(8,128)(2,1)} %fusion.11), calls=%async_computation.5 | async-start | bytes 262144 | tf_op jit(solution)/shard_map/all_to_all | solution.py:62
  182.1 7.6 %copy-start.2 = (bf16[1024,128]{1,0:T(8,128)(2,1)}, bf16[1024,128]{1,0:T(8,128)(2,1)S(1)}, u32[]{:S(2)}) copy-start(bf16[1024,128]{1,0:T(8,128)(2,1)S(1)} %copy.26) | copy-start | bytes 786436
  187.9 1.9 copy-start.6
  189.7 38.4 %all-to-all-start.4 = ((bf16[16,8,128,64]{2,3,1,0:T(8,128)(2,1)}), bf16[16,8,128,64]{2,3,1,0:T(8,128)(2,1)S(1)}, u32[]{:S(2)}, u32[]{:S(2)}) async-start(bf16[16,8,128,64]{2,3,1,0:T(8,128)(2,1)} %broadcast_in_dim.46), calls=%async_computation.4 | async-start | bytes 4194304 | tf_op jit(solution)/shard_map/all_to_all | solution.py:17
  228.2 1.0 copy-start.5
  228.2 1.3 copy-start.3
  228.2 1.3 copy-start.4
Sparse Core Ops, SparseCore 0:
  107.9 73.0 reduce-scatter.3
